TPU v7x, 512 devices: a whole 4x8x8 slice. The times are simulated.
512 devices in a mesh: rows: 64 (over y, x, core), grp: 8 (over z).
Axes of the slice: x: 4, y: 8, z: 8, core: 2. Of those that a mesh axis runs over, the one named last changes fastest.
Arguments:
- features: bfloat16 [524288, 256], P(('rows', 'grp')), may hold values from -1 to 1
- targets: bfloat16 [524288, 2048], P(('rows', 'grp')), may hold values from -6 to 6
- ridge: float32 [256], replicated, may hold values from 0.5 to 4
Outputs:
- readout: float32 [2048, 256], P('rows')
- factor: float32 [256, 256], replicated
All inputs are finite; a program needn't handle non-finite values.
Results may differ from a plain program's by a relative error of at most 0.0003.
Values sent between devices are 32-bit elements; how exact they have to be, the bound alone decides.
A program may use at most 64 MiB of HBM per device.

v0:
```python
import jax
import jax.numpy as jnp
from jax import lax
from jax.sharding import PartitionSpec as P


def product(left, right):
    return jnp.dot(left, right, precision=lax.Precision.HIGHEST, preferred_element_type=jnp.float32)


def factor_pair(matrix):
    order = matrix.shape[0]
    if order == 1:
        root = jnp.sqrt(matrix)
        return (root, 1.0 / root)
    middle = order // 2
    upper_left, inv_left = factor_pair(matrix[:middle, :middle])
    upper_right = product(inv_left.T, matrix[:middle, middle:])
    trailing = matrix[middle:, middle:] - product(upper_right.T, upper_right)
    lower_right, inv_right = factor_pair(trailing)
    zeros_block = jnp.zeros((order - middle, middle), jnp.float32)
    whole = jnp.concatenate(
        (
            jnp.concatenate((upper_left, upper_right), axis=1),
            jnp.concatenate((zeros_block, lower_right), axis=1),
        ),
        axis=0,
    )
    corner = -product(product(inv_left, upper_right), inv_right)
    inverse = jnp.concatenate(
        (
            jnp.concatenate((inv_left, corner), axis=1),
            jnp.concatenate((zeros_block, inv_right), axis=1),
        ),
        axis=0,
    )
    return (whole, inverse)


def shards(features, targets, ridge):
    dims = (((0,), (0,)), ((), ()))
    gram_local = lax.dot_general(features, features, dims, preferred_element_type=jnp.float32)
    gram_total = lax.psum(gram_local, ("rows", "grp"))
    label_part = lax.psum_scatter(
        lax.dot_general(targets, features, dims, preferred_element_type=jnp.float32),
        "rows",
        scatter_dimension=0,
        tiled=True,
    )
    label_cross = lax.psum(label_part, "grp")
    factor, factor_inverse = factor_pair(gram_total + jnp.diag(ridge))
    halfway = product(label_cross, factor_inverse)
    readout = product(halfway, factor_inverse.T)
    return (readout, factor)


def solution(mesh):
    return jax.shard_map(
        shards,
        mesh=mesh,
        in_specs=(P(("rows", "grp"), None), P(("rows", "grp"), None), P()),
        out_specs=(P("rows", None), P()),
        check_vma=False,
    )
```

profile of v0, /device:TPU:1, one launch (start us, length us, event | category | flops | bytes accessed | tf_op | source)
XLA Modules:
  0.0 796.2 jit_solution(9627917942159189043)
XLA Ops:
  8.1 1.0 copy-done
  9.0 1.0 fusion.1742
  10.2 4.8 fusion.1741
  15.0 273.0 %all-reduce.256.cloned.1.call-done = f32[256,256]{1,0:T(8,128)} async-done(((f32[256,256]{1,0:T(8,128)}), f32[256,256]{1,0:T(8,128)}) %all-reduce.256.cloned.1.call-update) | async-done | bytes 262160 | tf_op jit(solution)/shard_map/psum | solution.py:43
  288.0 1.0 select_add_fusion
  299.1 0.7 fusion.1739
  306.2 0.7 fusion.1738
  309.9 0.7 fusion.1675
  313.1 0.7 fusion.1737
  317.7 0.7 fusion.1628
  331.6 0.7 fusion.1643
  350.2 0.7 fusion.1732
  357.0 0.7 fusion.1731
  361.1 0.7 fusion.1642
  364.3 0.7 fusion.1730
  368.1 0.7 fusion.1671
  375.9 0.7 fusion.1627
  385.8 0.7 fusion.1727
  390.1 0.7 fusion.1641
  419.3 0.7 fusion.1640
  422.6 0.7 fusion.1722
  433.7 0.7 fusion.1626
  437.0 0.7 fusion.1720
  465.8 0.7 fusion.1716
  469.5 0.7 fusion.1664
  476.7 0.7 fusion.1638
  483.7 0.7 fusion.1663
  494.7 0.7 fusion.1712
  498.4 0.7 fusion.1662
  501.6 0.7 fusion.1711
  524.9 0.7 fusion.1708
  528.6 0.7 fusion.1660
  535.7 0.7 fusion.1636
  546.0 0.7 fusion.1705
  550.5 0.7 fusion.1624
  560.6 0.7 fusion.1703
  564.7 0.7 fusion.1635
  574.5 0.7 fusion.1701
  586.3 0.7 fusion.1656
  593.5 0.7 fusion.1634
  596.8 0.7 fusion.1698
  600.6 0.7 fusion.1655
  603.8 0.7 fusion.1697
  608.4 0.7 fusion.1623
  615.2 0.7 fusion.1654
  618.5 0.7 fusion.1695
  625.9 0.7 fusion.1694
  629.6 0.7 fusion.1653
  632.8 0.7 fusion.1693
  641.5 0.7 fusion.1692
  645.1 0.7 fusion.1652
  655.4 0.7 fusion.1690
  666.3 0.7 fusion.1622
  673.2 0.7 fusion.1650
  676.5 0.7 fusion.1687
  680.5 0.7 fusion.1631
  712.9 0.7 fusion.1682
  716.5 0.7 fusion.1647
  719.7 0.7 fusion.1681
  734.2 0.7 fusion.1679
  738.3 0.7 fusion.1629
  764.1 0.8 fusion.29
  765.0 22.6 %psum.14 = f32[32,256]{1,0:T(8,128)S(1)} all-reduce(f32[32,256]{1,0:T(8,128)} %reduce-scatter.2.cloned.1.call-done), channel_id=1, replica_groups=mesh['rows'=64,'grp'=8] {'grp'}, use_global_device_ids=true, to_apply=%region_1.0 | all-reduce | flops 8192 | bytes 65536 | tf_op jit(solution)/shard_map/psum | solution.py:50
  787.8 1.0 fusion.1809
  (970 shorter events, 172.8 us)
Async XLA Ops:
  8.0 1.0 copy-start
  8.0 280.0 %all-reduce.256.cloned.1.call-start = ((), (), s32[]{:S(2)}) async-start(), calls=%async_computation.2 | async-start | bytes 524288 | tf_op jit(solution)/shard_map/psum | solution.py:43
  10.1 277.9 %copy-start.1 = (f32[256]{0:T(256)S(1)}, f32[256]{0:T(256)}, u32[]{:S(2)}) copy-start(f32[256]{0:T(256)} %param.5) | copy-start | bytes 3076
  10.1 754.8 %reduce-scatter.2.cloned.1.call-start = ((), (), s32[]{:S(2)}) async-start(), calls=%async_computation.1 | async-start | bytes 2129920 | tf_op jit(solution)/shard_map/reduce_scatter | solution.py:44
Sparse Core Ops, SparseCore 0:
  15.2 272.7 all-reduce.255
Sparse Core Ops, SparseCore 1:
  15.2 149.2 reduce-scatter.1
where the time goes:
time: 806 us; the launch traced here: 796 us
  between operations  279 us (35%)
  waiting for transfers between devices  273 us (34%)
  matrix products  101 us (13%)
  local copies, waits for them, and re-layouts  92.2 us (11%)
  other arithmetic  27.6 us (3%)
  blocking collectives  22.6 us (3%)
    psum x1, waiting for transfers between devices, shards(): gram_total = lax.psum(gram_local, ('rows', 'grp'))  273 us
    dot_general x510, matrix products, product(): jnp.dot(left, right, precision=lax.Precision.HIGHEST, preferred_element_t...  95.4 us
    slice x128, local copies, waits for them, and re-layouts, factor_pair(): upper_right = product(inv_left.T, matrix[:middle, middle:])  86.3 us
    psum x1, blocking collectives, shards(): label_cross = lax.psum(label_part, 'grp')  22.6 us
  transfers between devices with their start and end apart: 2, of which 1 were waited for; matrix products, arithmetic and copies ran while one was open for 27% of the time, Pallas kernels for 0%

commit v1 on v0

v1 whole, which is shorter than its diff:
```python
import functools
import jax, jax.numpy as jnp
from jax import lax
from jax.experimental import pallas as pl
from jax.experimental.pallas import tpu as pltpu
from jax.sharding import PartitionSpec as P

HI = lax.Precision.HIGHEST


def mm(a, b, ca=1, cb=0):
    return lax.dot_general(a, b, (((ca,), (cb,)), ((), ())), precision=HI, preferred_element_type=jnp.float32)

def rows8(v, i):
    return jnp.broadcast_to(v[i:i+1, :], (8, 128))

def lane(v, j):
    return jnp.broadcast_to(v[:, j:j+1], (8, 128))

def chol_block(a, u_ref, v_ref):
    lanes = lax.broadcasted_iota(jnp.int32, (8, 128), 1)
    subs = lax.broadcasted_iota(jnp.int32, (8, 128), 0)
    a = list(a)
    e = [jnp.where(lanes == subs + 8 * g, 1.0, 0.0).astype(jnp.float32) for g in range(16)]
    for s in range(16):
        k = 8 * s
        cols = [[lane(a[g], k + j) for j in range(8)] for g in range(s, 16)]
        low = [[rows8(cols[0][j], i) for j in range(i + 1)] for i in range(8)]
        arow = [rows8(a[s], j) for j in range(8)]
        erow = [rows8(e[s], j) for j in range(8)]
        for j in range(8):
            r = lax.rsqrt(low[j][j])
            arow[j] = arow[j] * r
            erow[j] = erow[j] * r
            for i in range(j + 1, 8):
                low[i][j] = low[i][j] * r
            for g in range(1, 16 - s):
                cols[g][j] = cols[g][j] * r
            for i in range(j + 1, 8):
                l = low[i][j]
                for m in range(j + 1, i + 1):
                    low[i][m] = low[i][m] - l * low[m][j]
                arow[i] = arow[i] - l * arow[j]
                erow[i] = erow[i] - l * erow[j]
                for g in range(1, 16 - s):
                    cols[g][i] = cols[g][i] - l * cols[g][j]
            for g in range(1, 16 - s):
                a[s + g] = a[s + g] - cols[g][j] * arow[j]
                e[s + g] = e[s + g] - cols[g][j] * erow[j]
        uo, vo = arow[0], erow[0]
        for j in range(1, 8):
            uo = jnp.where(subs == j, arow[j], uo)
            vo = jnp.where(subs == j, erow[j], vo)
        u_ref[pl.ds(k, 8), :] = jnp.where(lanes >= subs + k, uo, 0.0)
        v_ref[pl.ds(k, 8), :] = jnp.where(lanes <= subs + k, vo, 0.0)

def chol_kernel(g_ref, ridge_ref, c_ref, out_ref, fac_ref, u1, v1, u2, v2, s22):
    lanes = lax.broadcasted_iota(jnp.int32, (8, 128), 1)
    subs = lax.broadcasted_iota(jnp.int32, (8, 128), 0)
    def ridged(g, half):
        rr = jnp.broadcast_to(ridge_ref[0:1, half * 128:half * 128 + 128], (8, 128))
        return lambda tile: tile + jnp.where(lanes == subs + 8 * g, rr, 0.0)
    a11 = [ridged(g, 0)(g_ref[g]) for g in range(16)]
    chol_block(a11, u1, v1)
    a12 = g_ref[16:32].reshape(128, 128)
    u12 = mm(v1[...], a12)
    s22[...] = mm(u12, u12, 0, 0)
    a22 = [ridged(g, 1)(g_ref[32 + g]) - s22[pl.ds(8 * g, 8), :] for g in range(16)]
    chol_block(a22, u2, v2)
    c1 = jnp.concatenate([c_ref[2 * t] for t in range(4)], axis=0)
    c2 = jnp.concatenate([c_ref[2 * t + 1] for t in range(4)], axis=0)
    x1 = mm(c1, v1[...], 1, 1)
    x2 = mm(c2 - mm(x1, u12), v2[...], 1, 1)
    y2 = mm(x2, v2[...])
    y1 = mm(x1 - mm(y2, u12, 1, 1), v1[...])
    out_ref[:, 0:128] = y1
    out_ref[:, 128:256] = y2
    fac_ref[0:128, 0:128] = u1[...]
    fac_ref[0:128, 128:256] = u12
    fac_ref[128:256, 0:128] = jnp.zeros((128, 128), jnp.float32)
    fac_ref[128:256, 128:256] = u2[...]

def chol_call(g, ridge, c):
    sq = pltpu.VMEM((128, 128), jnp.float32)
    vm = pl.BlockSpec(memory_space=pltpu.VMEM)
    return pl.pallas_call(chol_kernel,
        out_shape=(jax.ShapeDtypeStruct((32, 256), jnp.float32), jax.ShapeDtypeStruct((256, 256), jnp.float32)),
        in_specs=[vm, vm, vm], out_specs=(vm, vm),
        scratch_shapes=[sq] * 5)(g, ridge, c)

MESH = pl.DeviceIdType.MESH
LANES = 128


class Place:
    def __init__(self, n, nx):
        self.n, self.nx = n, nx
        rows, self.z = lax.axis_index("rows"), lax.axis_index("grp")
        self.c = rows % 2
        self.x = (rows // 2) % nx
        self.y = rows // (2 * nx)
        self.a = self.y + self.c * (self.z - self.y)
        self.b = self.z + self.c * (self.y - self.z)

    def device(self, y, x, c, z):
        return ((y * self.nx + x) * 2 + c, z)

    def partner(self):
        return self.device(self.y, self.x, 1 - self.c, self.z)

    def on_a(self, p):
        return self.device(p + self.c * (self.y - p), self.x, self.c, self.z + self.c * (p - self.z))

    def on_b(self, p):
        return self.device(self.y + self.c * (p - self.y), self.x, self.c, p + self.c * (self.z - p))

    def on_x(self, p):
        return self.device(self.y, p, self.c, self.z)

    def on_z(self, p):
        return self.device(self.y, self.x, self.c, p)


def far_first(n):
    return sorted(range(1, n), key=lambda d: -min(d, n - d))


def near_first(n):
    return sorted(range(1, n), key=lambda d: min(d, n - d))


def comm_kernel(
    n, nx, cross_ref, g_ref, gout, cout,
    rc, rg, hg, g1, g2, g3, h, b1, s1, b2, s2, b3,
    pair_send, pair_recv, gs1, gr1, gs2, gr2, gs3, gr3, gs4, gr4, gs5, gr5,
    cs1, cr1, cs2, cr2, cs3, cr3, cs4, cr4,
):
    me = Place(n, nx)
    c = me.c
    gt, tz, half = 24 // n, 8 // n, 24
    sends = []

    def send(src, dst, ssem, rsem, device):
        copy = pltpu.make_async_remote_copy(
            src_ref=src, dst_ref=dst, send_sem=ssem, recv_sem=rsem, device_id=device, device_id_type=MESH
        )
        copy.start()
        sends.append(copy)

    def arrived(dst, rsem):
        pltpu.make_async_copy(dst, dst, rsem).wait()

    barrier = pltpu.get_barrier_semaphore()
    greet = [me.partner()]
    greet += [me.on_a((me.a + d) % n) for d in range(1, n)]
    greet += [me.on_b((me.b + d) % n) for d in range(1, n)]
    greet += [me.on_x((me.x + d) % nx) for d in range(1, nx)]
    for device in greet:
        pl.semaphore_signal(barrier, inc=1, device_id=device, device_id_type=MESH)
    pl.semaphore_wait(barrier, len(greet))

    send(g_ref.at[pl.ds((1 - c) * half, half)], rg, pair_send.at[0], pair_recv.at[0], me.partner())
    send(cross_ref.at[:, 1 - c], rc, pair_send.at[1], pair_recv.at[1], me.partner())

    arrived(rg, pair_recv.at[0])
    for p in range(n):
        hg[p] = g_ref[pl.ds(c * half + p * gt, gt)] + rg[pl.ds(p * gt, gt)]
    for d in far_first(n):
        p = (me.a + d) % n
        send(hg.at[p], g1.at[me.a], gs1.at[d], gr1.at[me.a], me.on_a(p))
    g1[me.a] = hg[me.a]

    arrived(rc, pair_recv.at[1])

    def fill(blk, carry):
        y, x = blk // nx, blk % nx
        for q in range(8):
            rt, lh = q // 2, q % 2
            z, t = q // tz, q % tz
            at = (pl.ds(8 * rt, 8), pl.ds(LANES * lh, LANES))
            h[y + c * (z - y), x, z + c * (y - z), t] = cross_ref[(blk, c) + at] + rc[(blk,) + at]
        return carry

    lax.fori_loop(0, n * nx, fill, 0)
    for d in far_first(n):
        p = (me.a + d) % n
        send(h.at[p], b1.at[me.a], cs1.at[d], cr1.at[me.a], me.on_a(p))

    for d in near_first(n):
        p = (me.a + d) % n
        arrived(g1.at[p], gr1.at[p])
    g2[me.x] = sum_slots(g1, n)
    for d in far_first(nx):
        send(g2.at[me.x], g2.at[me.x], gs2.at[d], gr2.at[me.x], me.on_x((me.x + d) % nx))
    for d in near_first(nx):
        p = (me.x + d) % nx
        arrived(g2.at[p], gr2.at[p])
    g3[me.b] = sum_slots(g2, nx)
    for d in far_first(n):
        send(g3.at[me.b], g3.at[me.b], gs3.at[d], gr3.at[me.b], me.on_b((me.b + d) % n))
    for d in near_first(n):
        p = (me.b + d) % n
        arrived(g3.at[p], gr3.at[p])

    def owned(p):
        return pl.ds(c * half + p * gt, gt)

    gout[owned(me.a)] = sum_slots(g3, n)
    for d in far_first(n):
        send(gout.at[owned(me.a)], gout.at[owned(me.a)], gs4.at[d], gr4.at[me.a], me.on_a((me.a + d) % n))
    send(gout.at[owned(me.a)], gout.at[owned(me.a)], gs5.at[me.a], gr5.at[me.a], me.partner())
    for d in near_first(n):
        p = (me.a + d) % n
        arrived(gout.at[owned(p)], gr4.at[p])
        send(gout.at[owned(p)], gout.at[owned(p)], gs5.at[p], gr5.at[p], me.partner())

    for d in near_first(n):
        p = (me.a + d) % n
        arrived(b1.at[p], cr1.at[p])

    def add1(x, carry):
        total = h[me.a, x]
        for d in range(1, n):
            total = total + b1[(me.a + d) % n, x]
        s1[x] = total
        return carry

    lax.fori_loop(0, nx, add1, 0)
    for d in far_first(nx):
        p = (me.x + d) % nx
        send(s1.at[p], b2.at[me.x], cs2.at[d], cr2.at[me.x], me.on_x(p))
    for d in near_first(nx):
        p = (me.x + d) % nx
        arrived(b2.at[p], cr2.at[p])
    total = s1[me.x]
    for d in range(1, nx):
        total = total + b2[(me.x + d) % nx]
    s2[...] = total
    for d in far_first(n):
        p = (me.b + d) % n
        send(s2.at[p], b3.at[me.b], cs3.at[d], cr3.at[me.b], me.on_b(p))
    for d in near_first(n):
        p = (me.b + d) % n
        arrived(b3.at[p], cr3.at[p])
    total = s2[me.b]
    for d in range(1, n):
        total = total + b3[(me.b + d) % n]
    mine = pl.ds(me.z * tz, tz)
    cout[mine] = total
    for d in far_first(n):
        send(cout.at[mine], cout.at[mine], cs4.at[d], cr4.at[me.z], me.on_z((me.z + d) % n))
    for p in range(n):
        pass
    for d in near_first(n):
        p = (me.z + d) % n
        arrived(cout.at[pl.ds(p * tz, tz)], cr4.at[p])
    for p in range(n):
        arrived(gout.at[pl.ds((1 - c) * half + p * gt, gt)], gr5.at[p])
    for copy in sends:
        copy.wait_send()


def sum_slots(ref, count):
    total = ref[0]
    for p in range(1, count):
        total = total + ref[p]
    return total


def comm_call(n, nx, cross, g):
    gt, tz = 24 // n, 8 // n
    f32 = lambda *lead: pltpu.VMEM(lead + (8, LANES), jnp.float32)
    dma = lambda k: pltpu.SemaphoreType.DMA((k,))
    vmem = pl.BlockSpec(memory_space=pltpu.VMEM)
    return pl.pallas_call(
        functools.partial(comm_kernel, n, nx),
        out_shape=(
            jax.ShapeDtypeStruct((48, 8, LANES), jnp.float32),
            jax.ShapeDtypeStruct((8, 8, LANES), jnp.float32),
        ),
        in_specs=[vmem, vmem],
        out_specs=(vmem, vmem),
        scratch_shapes=[
            pltpu.VMEM((n * nx, 32, 256), jnp.float32), f32(24), f32(n, gt), f32(n, gt), f32(nx, gt), f32(n, gt),
            f32(n, nx, n, tz), f32(n, nx, n, tz), f32(nx, n, tz), f32(nx, n, tz), f32(n, tz), f32(n, tz),
            dma(2), dma(2), dma(n), dma(n), dma(nx), dma(nx), dma(n), dma(n), dma(n), dma(n), dma(n), dma(n),
            dma(n), dma(n), dma(nx), dma(nx), dma(n), dma(n), dma(n), dma(n),
        ],
        compiler_params=pltpu.CompilerParams(collective_id=0, has_side_effects=True),
    )(cross, g)


def shards(n, nx, features, targets, ridge):
    dims = (((0,), (0,)), ((), ()))
    gram = lax.dot_general(features, features, dims, preferred_element_type=jnp.float32)
    cross = lax.dot_general(targets, features, dims, preferred_element_type=jnp.float32)
    tiles = jnp.concatenate([gram[:128, :128], gram[:128, 128:], gram[128:, 128:]], axis=0).reshape(48, 8, LANES)
    g, c = comm_call(n, nx, cross.reshape(n * nx, 2, 32, 256), tiles)
    return chol_call(g, ridge.reshape(1, 256), c)


def solution(mesh):
    n = mesh.shape["grp"]
    nx = mesh.shape["rows"] // (2 * n)
    return jax.shard_map(
        functools.partial(shards, n, nx),
        mesh=mesh,
        in_specs=(P(("rows", "grp"), None), P(("rows", "grp"), None), P()),
        out_specs=(P("rows", None), P()),
        check_vma=False,
    )
```

time: 806 us -> 71.1 us (0.09); the launches traced: 796 us -> 70.2 us
  between operations: 279 us -> 0.67 us
  waiting for transfers between devices: 273 us -> 0 us
  matrix products: 101 us -> 5.17 us
  local copies, waits for them, and re-layouts: 92.2 us -> 1.06 us
  Pallas kernels: 0 us -> 62.6 us
  other arithmetic: 27.6 us -> 0.69 us
  blocking collectives: 22.6 us -> 0 us
    psum x1 -> x0, waiting for transfers between devices: 273 us -> none  [shards(): gram_total = lax.psum(gram_local, ('rows', 'grp'))]
    dot_general x510 -> x0, matrix products: 95.4 us -> none  [product(): jnp.dot(left, right, precision=lax.Precision.HIGHEST, preferred_element_t...]
    slice x128 -> x2, local copies, waits for them, and re-layouts: 86.3 us -> 0.02 us  [the longest x1 0.01 us: shards(): gram[:128, 128:]]
    pallas_call x0 -> x2, Pallas kernels: none -> 62.6 us  [the longest x1 50.2 us: comm_call(): pl.pallas_call(functools.partial(comm_kernel, n, nx), out_shape=(jax.Shap...]
    concatenate x318 -> x0, other arithmetic: 26.5 us -> none  [the longest x193 15.8 us: factor_pair(): jnp.concatenate((jnp.concatenate((inv_left, corner), axis=1), jnp.concate...]
    psum x1 -> x0, blocking collectives: 22.6 us -> none  [shards(): label_cross = lax.psum(label_part, 'grp')]
  transfers between devices with their start and end apart: 2 -> 0, of which waited for: 1 -> 0; matrix products, arithmetic and copies ran while one was open for 27% -> 0% of each run, Pallas kernels for 0% -> 0%
where the time goes in v1:
time: 71.1 us; the launch traced here: 70.2 us
  Pallas kernels  62.6 us (88%)
  matrix products  5.17 us (7%)
  local copies, waits for them, and re-layouts  1.06 us (1%)
    pallas_call x1, Pallas kernels, comm_call(): pl.pallas_call(functools.partial(comm_kernel, n, nx), out_shape=(jax.Shap...  50.2 us
    pallas_call x1, Pallas kernels, chol_call(): pl.pallas_call(chol_kernel, out_shape=(jax.ShapeDtypeStruct((32, 256), jn...  12.4 us
    dot_general x1, matrix products, shards(): lax.dot_general(targets, features, dims, preferred_element_type=jnp.float32)  4.84 us

profile of v1, /device:TPU:1, one launch (start us, length us, event | category | flops | bytes accessed | tf_op | source)
XLA Modules:
  0.0 70.2 jit_solution(3435448176450310056)
XLA Ops:
  0.6 0.0 copy-start
  0.6 1.0 %copy-done = bf16[1024,256]{1,0:T(8,128)(2,1)S(1)} copy-done((bf16[1024,256]{1,0:T(8,128)(2,1)S(1)}, bf16[1024,256]{1,0:T(8,128)(2,1)}, u32[]{:S(2)}) %copy-start) | copy-done | bytes 524312
  1.7 0.3 fusion.1
  2.1 0.7 maximum_bitcast_fusion.g_ref
  2.7 4.8 %fusion = f32[2048,256]{1,0:T(8,128)} fusion(bf16[1024,2048]{1,0:T(8,128)(2,1)} %param.4, bf16[1024,256]{1,0:T(8,128)(2,1)S(1)} %copy-done), kind=kOutput, calls=%fused_computation.1 | convolution fusion | flops 1073741824 | bytes 6815744 | tf_op jit(solution)/shard_map/dot_general | solution.py:296
  7.6 50.2 %shard_map.50 = (f32[48,8,128]{2,1,0:T(8,128)}, f32[8,8,128]{2,1,0:T(8,128)}) custom-call(f32[32,2,32,256]{3,2,1,0:T(8,128)} %bitcast.8, f32[48,8,128]{2,1,0:T(8,128)} %maximum_bitcast_fusion.g_ref), custom_call_target="tpu_custom_call" | custom-call | tf_op jit(solution)/shard_map/pallas_call | solution.py:275
  57.8 12.4 %shard_map.51 = (f32[32,256]{1,0:T(8,128)}, f32[256,256]{1,0:T(8,128)}) custom-call(f32[48,8,128]{2,1,0:T(8,128)} %get-tuple-element.4.g_ref, f32[1,256]{1,0:T(1,128)} %bitcast.9, f32[8,8,128]{2,1,0:T(8,128)} %get-tuple-element.5.c_ref), custom_call_target="tpu_custom_call" | custom-call | tf_op jit(solution)/shard_map/pallas_call | solution.py:86
  (2 shorter events, 0.0 us)
Async XLA Ops:
  0.6 1.0 %copy-start = (bf16[1024,256]{1,0:T(8,128)(2,1)S(1)}, bf16[1024,256]{1,0:T(8,128)(2,1)}, u32[]{:S(2)}) copy-start(bf16[1024,256]{1,0:T(8,128)(2,1)} %param.3) | copy-start | bytes 1572868

commit v2 on v1

v2 whole, which is shorter than its diff:
```python
import functools
import jax, jax.numpy as jnp
from jax import lax
from jax.experimental import pallas as pl
from jax.experimental.pallas import tpu as pltpu
from jax.sharding import PartitionSpec as P

HI = lax.Precision.HIGHEST


def mm(a, b, ca=1, cb=0):
    return lax.dot_general(a, b, (((ca,), (cb,)), ((), ())), precision=HI, preferred_element_type=jnp.float32)

def rows8(v, i):
    return jnp.broadcast_to(v[i:i+1, :], (8, 128))

def lane(v, j):
    return jnp.broadcast_to(v[:, j:j+1], (8, 128))

def chol_block(a, u_ref, v_ref, base, hooks):
    lanes = lax.broadcasted_iota(jnp.int32, (8, 128), 1)
    subs = lax.broadcasted_iota(jnp.int32, (8, 128), 0)
    a = list(a)
    e = [jnp.where(lanes == subs + 8 * g, 1.0, 0.0).astype(jnp.float32) for g in range(16)]
    for s in range(16):
        k = 8 * s
        if s in hooks:
            hooks[s]()
        cols = [[lane(a[g], k + j) for j in range(8)] for g in range(s, 16)]
        low = [[rows8(cols[0][j], i) for j in range(i + 1)] for i in range(8)]
        arow = [rows8(a[s], j) for j in range(8)]
        erow = [rows8(e[s], j) for j in range(8)]
        for j in range(8):
            r = lax.rsqrt(low[j][j])
            arow[j] = arow[j] * r
            erow[j] = erow[j] * r
            for i in range(j + 1, 8):
                low[i][j] = low[i][j] * r
            for g in range(1, 16 - s):
                cols[g][j] = cols[g][j] * r
            for i in range(j + 1, 8):
                l = low[i][j]
                for m in range(j + 1, i + 1):
                    low[i][m] = low[i][m] - l * low[m][j]
                arow[i] = arow[i] - l * arow[j]
                erow[i] = erow[i] - l * erow[j]
                for g in range(1, 16 - s):
                    cols[g][i] = cols[g][i] - l * cols[g][j]
            for g in range(1, 16 - s):
                a[s + g] = a[s + g] - cols[g][j] * arow[j]
                e[s + g] = e[s + g] - cols[g][j] * erow[j]
        uo, vo = arow[0], erow[0]
        for j in range(1, 8):
            uo = jnp.where(subs == j, arow[j], uo)
            vo = jnp.where(subs == j, erow[j], vo)
        u_ref[pl.ds(base + k, 8), pl.ds(base, 128)] = jnp.where(lanes >= subs + k, uo, 0.0)
        v_ref[pl.ds(base + k, 8), pl.ds(base, 128)] = jnp.where(lanes <= subs + k, vo, 0.0)

MESH = pl.DeviceIdType.MESH
LANES = 128


class Place:
    def __init__(self, n, nx):
        self.n, self.nx = n, nx
        rows, self.z = lax.axis_index("rows"), lax.axis_index("grp")
        self.c = rows % 2
        self.x = (rows // 2) % nx
        self.y = rows // (2 * nx)
        self.a = self.y + self.c * (self.z - self.y)
        self.b = self.z + self.c * (self.y - self.z)

    def device(self, y, x, c, z):
        return ((y * self.nx + x) * 2 + c, z)

    def partner(self):
        return self.device(self.y, self.x, 1 - self.c, self.z)

    def on_a(self, p):
        return self.device(p + self.c * (self.y - p), self.x, self.c, self.z + self.c * (p - self.z))

    def on_b(self, p):
        return self.device(self.y + self.c * (p - self.y), self.x, self.c, p + self.c * (self.z - p))

    def on_x(self, p):
        return self.device(self.y, p, self.c, self.z)

    def on_z(self, p):
        return self.device(self.y, self.x, self.c, p)


def far_first(n):
    return sorted(range(1, n), key=lambda d: -min(d, n - d))


def near_first(n):
    return sorted(range(1, n), key=lambda d: min(d, n - d))


def sum_slots(ref, count):
    total = ref[0]
    for p in range(1, count):
        total = total + ref[p]
    return total


def ridge_kernel(
    n, nx, f_hbm, t_hbm, ridge_ref, out_ref, fac_ref,
    feat, targ, cross, gram, gsum, csum, v_ref, q_ref,
    rc, rg, hg, g1, g2, g3, h, b1, s1, b2, s2, b3,
    load, gpair_s, gpair_r, cpair_s, cpair_r,
    gs1, gr1, gs2, gr2, gs3, gr3, gs4, gr4, gs5, gr5,
    cs1, cr1, cs2, cr2, cs3, cr3, cs4, cr4,
):
    me = Place(n, nx)
    c = me.c
    gt, tz, half = 24 // n, 8 // n, 24
    width = nx * 64
    sends = []

    def remote(src, dst, ssem, rsem, device):
        return pltpu.make_async_remote_copy(
            src_ref=src, dst_ref=dst, send_sem=ssem, recv_sem=rsem, device_id=device, device_id_type=MESH
        )

    def send(*what):
        copy = remote(*what)
        copy.start()
        sends.append(copy)

    def arrived(dst, rsem):
        pltpu.make_async_copy(dst, dst, rsem).wait()

    def columns(y):
        return pl.ds(pl.multiple_of(y * width, width), width)

    def load_targets(y):
        return pltpu.make_async_copy(t_hbm.at[:, columns(y)], targ.at[y], load.at[y])

    load_features = pltpu.make_async_copy(f_hbm, feat, load.at[n])
    load_features.start()
    for y in range(n):
        load_targets(y).start()

    barrier = pltpu.get_barrier_semaphore()
    greet = [me.partner()]
    greet += [me.on_a((me.a + d) % n) for d in far_first(n)]
    greet += [me.on_b((me.b + d) % n) for d in far_first(n)]
    greet += [me.on_x((me.x + d) % nx) for d in far_first(nx)]
    for device in greet:
        pl.semaphore_signal(barrier, inc=1, device_id=device, device_id_type=MESH)

    over_rows = (((0,), (0,)), ((), ()))
    load_features.wait()
    whole = lax.dot_general(feat[...], feat[...], over_rows, preferred_element_type=jnp.float32)
    gram[0:16] = whole[0:128, 0:128].reshape(16, 8, LANES)
    gram[16:32] = whole[0:128, 128:256].reshape(16, 8, LANES)
    gram[32:48] = whole[128:256, 128:256].reshape(16, 8, LANES)
    pl.semaphore_wait(barrier, len(greet))
    send(gram.at[pl.ds((1 - c) * half, half)], rg, gpair_s, gpair_r, me.partner())

    def pair(y):
        at = pl.ds(y * nx, nx)
        return remote(cross.at[at, 1 - c], rc.at[at], cpair_s.at[y], cpair_r.at[y], me.partner())

    def multiply(y, carry):
        load_targets(y).wait()
        block = lax.dot_general(targ[y], feat[...], over_rows, preferred_element_type=jnp.float32)
        cross[pl.ds(y * nx, nx)] = block.reshape(nx, 2, 32, 256)
        pair(y).start()
        return carry

    lax.fori_loop(0, n // 2, multiply, 0)
    arrived(rg, gpair_r)
    for p in range(n):
        hg[p] = gram[pl.ds(c * half + p * gt, gt)] + rg[pl.ds(p * gt, gt)]
    for d in far_first(n):
        p = (me.a + d) % n
        send(hg.at[p], g1.at[me.a], gs1.at[d], gr1.at[me.a], me.on_a(p))
    g1[me.a] = hg[me.a]
    lax.fori_loop(n // 2, n, multiply, 0)

    def fill(y, carry):
        arrived(rc.at[pl.ds(y * nx, nx)], cpair_r.at[y])
        for x in range(nx):
            blk = y * nx + x
            for q in range(8):
                rt, lh = q // 2, q % 2
                z, t = q // tz, q % tz
                at = (pl.ds(8 * rt, 8), pl.ds(LANES * lh, LANES))
                h[y + c * (z - y), x, z + c * (y - z), t] = cross[(blk, c) + at] + rc[(blk,) + at]
        return carry

    lax.fori_loop(0, n, fill, 0)
    for d in far_first(n):
        p = (me.a + d) % n
        send(h.at[p], b1.at[me.a], cs1.at[d], cr1.at[me.a], me.on_a(p))

    for d in near_first(n):
        p = (me.a + d) % n
        arrived(g1.at[p], gr1.at[p])
    g2[me.x] = sum_slots(g1, n)
    for d in far_first(nx):
        send(g2.at[me.x], g2.at[me.x], gs2.at[d], gr2.at[me.x], me.on_x((me.x + d) % nx))
    for d in near_first(nx):
        p = (me.x + d) % nx
        arrived(g2.at[p], gr2.at[p])
    g3[me.b] = sum_slots(g2, nx)
    for d in far_first(n):
        send(g3.at[me.b], g3.at[me.b], gs3.at[d], gr3.at[me.b], me.on_b((me.b + d) % n))
    for d in near_first(n):
        p = (me.b + d) % n
        arrived(g3.at[p], gr3.at[p])

    def owned(p):
        return pl.ds(c * half + p * gt, gt)

    gsum[owned(me.a)] = sum_slots(g3, n)
    for d in far_first(n):
        send(gsum.at[owned(me.a)], gsum.at[owned(me.a)], gs4.at[d], gr4.at[me.a], me.on_a((me.a + d) % n))
    send(gsum.at[owned(me.a)], gsum.at[owned(me.a)], gs5.at[me.a], gr5.at[me.a], me.partner())
    for d in near_first(n):
        p = (me.a + d) % n
        arrived(gsum.at[owned(p)], gr4.at[p])
        send(gsum.at[owned(p)], gsum.at[owned(p)], gs5.at[p], gr5.at[p], me.partner())
    for p in range(n):
        arrived(gsum.at[pl.ds((1 - c) * half + p * gt, gt)], gr5.at[p])

    def sum_a():
        for d in near_first(n):
            p = (me.a + d) % n
            arrived(b1.at[p], cr1.at[p])

        def add(x, carry):
            total = h[me.a, x]
            for d in range(1, n):
                total = total + b1[(me.a + d) % n, x]
            s1[x] = total
            return carry

        lax.fori_loop(0, nx, add, 0)
        for d in far_first(nx):
            p = (me.x + d) % nx
            send(s1.at[p], b2.at[me.x], cs2.at[d], cr2.at[me.x], me.on_x(p))

    def sum_x():
        total = s1[me.x]
        for d in near_first(nx):
            p = (me.x + d) % nx
            arrived(b2.at[p], cr2.at[p])
            total = total + b2[p]
        s2[...] = total
        for d in far_first(n):
            p = (me.b + d) % n
            send(s2.at[p], b3.at[me.b], cs3.at[d], cr3.at[me.b], me.on_b(p))

    mine = pl.ds(me.z * tz, tz)

    def sum_b():
        total = s2[me.b]
        for d in near_first(n):
            p = (me.b + d) % n
            arrived(b3.at[p], cr3.at[p])
            total = total + b3[p]
        csum[mine] = total
        for d in far_first(n):
            send(csum.at[mine], csum.at[mine], cs4.at[d], cr4.at[me.z], me.on_z((me.z + d) % n))

    lanes = lax.broadcasted_iota(jnp.int32, (8, 128), 1)
    subs = lax.broadcasted_iota(jnp.int32, (8, 128), 0)

    def ridged(tile, g, start):
        values = jnp.broadcast_to(ridge_ref[0:1, start:start + 128], (8, 128))
        return tile + jnp.where(lanes == subs + 8 * g, values, 0.0)

    chol_block([ridged(gsum[g], g, 0) for g in range(16)], fac_ref, v_ref, 0, first_hooks(sum_a, sum_x, sum_b))
    v11 = v_ref[0:128, 0:128]
    u12 = mm(v11, gsum[16:32].reshape(128, 128))
    fac_ref[0:128, 128:256] = u12
    fac_ref[128:256, 0:128] = jnp.zeros((128, 128), jnp.float32)
    v_ref[0:128, 128:256] = jnp.zeros((128, 128), jnp.float32)
    q_ref[0] = mm(u12, u12, 0, 0)
    q_ref[1] = mm(u12, v11, 0, 0)
    trailing = [ridged(gsum[32 + g], g, 128) - q_ref[0, pl.ds(8 * g, 8), :] for g in range(16)]
    chol_block(trailing, fac_ref, v_ref, 128, second_hooks(sum_a, sum_x, sum_b))
    v_ref[128:256, 0:128] = -mm(v_ref[128:256, 128:256], q_ref[1])

    for d in near_first(n):
        p = (me.z + d) % n
        arrived(csum.at[pl.ds(p * tz, tz)], cr4.at[p])
    left = jnp.concatenate([csum[2 * t] for t in range(4)], axis=0)
    right = jnp.concatenate([csum[2 * t + 1] for t in range(4)], axis=0)
    halfway = mm(jnp.concatenate([left, right], axis=1), v_ref[...], 1, 1)
    out_ref[...] = mm(halfway, v_ref[...])

    def sent(y, carry):
        pair(y).wait_send()
        return carry

    lax.fori_loop(0, n, sent, 0)
    for copy in sends:
        copy.wait_send()


def first_hooks(sum_a, sum_x, sum_b):
    return {2: sum_a, 13: sum_x}


def second_hooks(sum_a, sum_x, sum_b):
    return {6: sum_b}


def ridge_call(n, nx, features, targets, ridge):
    gt, tz = 24 // n, 8 // n
    rows = features.shape[0]
    f32 = lambda *shape: pltpu.VMEM(shape, jnp.float32)
    tiles = lambda *lead: f32(*lead, 8, LANES)
    dma = lambda k: pltpu.SemaphoreType.DMA((k,))
    one = pltpu.SemaphoreType.DMA
    vmem, hbm = pl.BlockSpec(memory_space=pltpu.VMEM), pl.BlockSpec(memory_space=pltpu.HBM)
    return pl.pallas_call(
        functools.partial(ridge_kernel, n, nx),
        out_shape=(
            jax.ShapeDtypeStruct((32, 256), jnp.float32),
            jax.ShapeDtypeStruct((256, 256), jnp.float32),
        ),
        in_specs=[hbm, hbm, vmem],
        out_specs=(vmem, vmem),
        scratch_shapes=[
            pltpu.VMEM((rows, 256), jnp.bfloat16), pltpu.VMEM((n, rows, nx * 64), jnp.bfloat16),
            f32(n * nx, 2, 32, 256), tiles(48), tiles(48), tiles(8), f32(256, 256), f32(2, 128, 128),
            f32(n * nx, 32, 256), tiles(24), tiles(n, gt), tiles(n, gt), tiles(nx, gt), tiles(n, gt),
            tiles(n, nx, n, tz), tiles(n, nx, n, tz), tiles(nx, n, tz), tiles(nx, n, tz), tiles(n, tz), tiles(n, tz),
            dma(n + 1), one, one, dma(n), dma(n),
            dma(n), dma(n), dma(nx), dma(nx), dma(n), dma(n), dma(n), dma(n), dma(n), dma(n),
            dma(n), dma(n), dma(nx), dma(nx), dma(n), dma(n), dma(n), dma(n),
        ],
        compiler_params=pltpu.CompilerParams(collective_id=0, has_side_effects=True),
    )(features, targets, ridge)


def shards(n, nx, features, targets, ridge):
    return ridge_call(n, nx, features, targets, ridge.reshape(1, 256))


def solution(mesh):
    n = mesh.shape["grp"]
    nx = mesh.shape["rows"] // (2 * n)
    return jax.shard_map(
        functools.partial(shards, n, nx),
        mesh=mesh,
        in_specs=(P(("rows", "grp"), None), P(("rows", "grp"), None), P()),
        out_specs=(P("rows", None), P()),
        check_vma=False,
    )
```

time: 71.1 us -> 57.6 us (0.81)
  Pallas kernels: 62.6 us -> 53.7 us
  matrix products: 5.17 us -> 0 us
  local copies, waits for them, and re-layouts: 1.06 us -> 3.04 us
    pallas_call x2 -> x1, Pallas kernels: 62.6 us -> 53.7 us  [ridge_call(): pl.pallas_call(functools.partial(ridge_kernel, n, nx), out_shape=(jax.Sha...]
    dot_general x2 -> x0, matrix products: 5.17 us -> none  [the longest x1 4.84 us: shards(): lax.dot_general(targets, features, dims, preferred_element_type=jnp.float32)]
    unnamed x2, local copies, waits for them, and re-layouts: 1.04 us -> 3.04 us
where the time goes in v2:
time: 57.6 us; the launch traced here: 57.4 us
  Pallas kernels  53.7 us (93%)
  local copies, waits for them, and re-layouts  3.04 us (5%)
  between operations  0.64 us (1%)
    pallas_call x1, Pallas kernels, ridge_call(): pl.pallas_call(functools.partial(ridge_kernel, n, nx), out_shape=(jax.Sha...  53.7 us
    unnamed x2, local copies, waits for them, and re-layouts  3.04 us

profile of v2, /device:TPU:1, one launch (start us, length us, event | category | flops | bytes accessed | tf_op | source)
XLA Modules:
  0.0 57.4 jit_solution(17372507750199769262)
XLA Ops:
  0.6 53.7 %shard_map.50 = (f32[32,256]{1,0:T(8,128)}, f32[256,256]{1,0:T(8,128)}) custom-call(bf16[1024,256]{1,0:T(8,128)(2,1)} %f_hbm.1, bf16[1024,2048]{1,0:T(8,128)(2,1)} %t_hbm.1, f32[1,256]{1,0:T(1,128)} %bitcast.1), custom_call_target="tpu_custom_call" | custom-call | tf_op jit(solution)/shard_map/pallas_call | solution.py:321
  54.4 1.4 %copy.7 = f32[32,256]{1,0:T(8,128)} copy(f32[32,256]{1,0:T(8,128)} %get-tuple-element.4) | data formatting | bytes 65536
  55.7 1.7 %copy.8 = f32[256,256]{1,0:T(8,128)} copy(f32[256,256]{1,0:T(8,128)} %get-tuple-element.5) | data formatting | bytes 524288

commit v3 on v2

--- a/solution.py
+++ b/solution.py
@@ -14,45 +14,72 @@
 def rows8(v, i):
     return jnp.broadcast_to(v[i:i+1, :], (8, 128))
 
-def lane(v, j):
-    return jnp.broadcast_to(v[:, j:j+1], (8, 128))
+def gl(v, j):
+    return jnp.take_along_axis(v, jnp.full((8, 128), j, jnp.int32), axis=1)
 
 def chol_block(a, u_ref, v_ref, base, hooks):
     lanes = lax.broadcasted_iota(jnp.int32, (8, 128), 1)
     subs = lax.broadcasted_iota(jnp.int32, (8, 128), 0)
-    a = list(a)
-    e = [jnp.where(lanes == subs + 8 * g, 1.0, 0.0).astype(jnp.float32) for g in range(16)]
+    m = list(a)
+
+    def spread(s):
+        arow = [rows8(m[s], j) for j in range(8)]
+        low = [[gl(arow[j], 8 * s + i) for j in range(i + 1)] for i in range(8)]
+        return arow, low
+
+    ahead = spread(0)
     for s in range(16):
         k = 8 * s
         if s in hooks:
             hooks[s]()
-        cols = [[lane(a[g], k + j) for j in range(8)] for g in range(s, 16)]
-        low = [[rows8(cols[0][j], i) for j in range(i + 1)] for i in range(8)]
-        arow = [rows8(a[s], j) for j in range(8)]
-        erow = [rows8(e[s], j) for j in range(8)]
+        inside = (lanes >= k) & (lanes < k + 8)
+        arow, low = ahead
+        near = [gl(m[s + 1], k + j) for j in range(8)] if s < 15 else None
+        mixed = jnp.where(inside, jnp.where(lanes == subs + k, 1.0, 0.0), m[s])
+        mrow = [rows8(mixed, j) for j in range(8)]
+        bycol = [[gl(m[g], k + j) for g in range(s + 2, 16)] for j in range(8)]
+        far = list(zip(*bycol))
+        if s < 15:
+            nxt = jnp.where(inside, 0.0, m[s + 1])
+        rs = []
         for j in range(8):
             r = lax.rsqrt(low[j][j])
-            arow[j] = arow[j] * r
-            erow[j] = erow[j] * r
+            rs.append(r)
             for i in range(j + 1, 8):
                 low[i][j] = low[i][j] * r
-            for g in range(1, 16 - s):
-                cols[g][j] = cols[g][j] * r
             for i in range(j + 1, 8):
-                l = low[i][j]
-                for m in range(j + 1, i + 1):
-                    low[i][m] = low[i][m] - l * low[m][j]
-                arow[i] = arow[i] - l * arow[j]
-                erow[i] = erow[i] - l * erow[j]
-                for g in range(1, 16 - s):
-                    cols[g][i] = cols[g][i] - l * cols[g][j]
-            for g in range(1, 16 - s):
-                a[s + g] = a[s + g] - cols[g][j] * arow[j]
-                e[s + g] = e[s + g] - cols[g][j] * erow[j]
-        uo, vo = arow[0], erow[0]
+                for t in range(j + 1, i + 1):
+                    low[i][t] = low[i][t] - low[i][j] * low[t][j]
+            mrow[j] = mrow[j] * r
+            for i in range(j + 1, 8):
+                mrow[i] = mrow[i] - low[i][j] * mrow[j]
+            if s < 15:
+                near[j] = near[j] * r
+                for i in range(j + 1, 8):
+                    near[i] = near[i] - low[i][j] * near[j]
+                nxt = nxt - near[j] * mrow[j]
+        if s < 15:
+            m[s + 1] = nxt
+            ahead = spread(s + 1)
+        if far:
+            w = list(mrow)
+            for j in reversed(range(8)):
+                w[j] = w[j] * rs[j]
+                for i in range(j):
+                    w[i] = w[i] - low[j][i] * w[j]
+            for g, cols in enumerate(far, start=s + 2):
+                out = jnp.where(inside, 0.0, m[g])
+                for j in range(8):
+                    out = out - cols[j] * w[j]
+                m[g] = out
+        for j in range(8):
+            arow[j] = arow[j] * rs[j]
+            for i in range(j + 1, 8):
+                arow[i] = arow[i] - low[i][j] * arow[j]
+        uo, vo = arow[0], mrow[0]
         for j in range(1, 8):
             uo = jnp.where(subs == j, arow[j], uo)
-            vo = jnp.where(subs == j, erow[j], vo)
+            vo = jnp.where(subs == j, mrow[j], vo)
         u_ref[pl.ds(base + k, 8), pl.ds(base, 128)] = jnp.where(lanes >= subs + k, uo, 0.0)
         v_ref[pl.ds(base + k, 8), pl.ds(base, 128)] = jnp.where(lanes <= subs + k, vo, 0.0)
 
@@ -107,10 +134,10 @@
 def ridge_kernel(
     n, nx, f_hbm, t_hbm, ridge_ref, out_ref, fac_ref,
     feat, targ, cross, gram, gsum, csum, v_ref, q_ref,
-    rc, rg, hg, g1, g2, g3, h, b1, s1, b2, s2, b3,
+    rc, rg, hg, g1, g2, g3, hx, bx1, sx, bx2, ha, ba1, sa, ba2, s2, b3,
     load, gpair_s, gpair_r, cpair_s, cpair_r,
     gs1, gr1, gs2, gr2, gs3, gr3, gs4, gr4, gs5, gr5,
-    cs1, cr1, cs2, cr2, cs3, cr3, cs4, cr4,
+    xs1, xr1, xs2, xr2, as1, ar1, as2, ar2, cs3, cr3, cs4, cr4,
 ):
     me = Place(n, nx)
     c = me.c
@@ -163,11 +190,50 @@
         at = pl.ds(y * nx, nx)
         return remote(cross.at[at, 1 - c], rc.at[at], cpair_s.at[y], cpair_r.at[y], me.partner())
 
-    def multiply(y, carry):
+    def turn(i):
+        return (me.y + n // 2 + i) % n
+
+    def multiply(i, carry):
+        y = turn(i)
         load_targets(y).wait()
         block = lax.dot_general(targ[y], feat[...], over_rows, preferred_element_type=jnp.float32)
         cross[pl.ds(y * nx, nx)] = block.reshape(nx, 2, 32, 256)
         pair(y).start()
+        return carry
+
+    def pass_on(i):
+        y = turn(i)
+        arrived(rc.at[pl.ds(y * nx, nx)], cpair_r.at[y])
+        for x in range(nx):
+            blk = y * nx + x
+            for q in range(8):
+                rt, lh = q // 2, q % 2
+                z, t = q // tz, q % tz
+                upper = (pl.ds(8 * rt, 4), pl.ds(LANES * lh, LANES))
+                lower = (pl.ds(8 * rt + 4, 4), pl.ds(LANES * lh, LANES))
+                hx[x, y, z, t] = cross[(blk, c) + upper] + rc[(blk,) + upper]
+                ha[y + c * (z - y), z + c * (y - z), x, t] = cross[(blk, c) + lower] + rc[(blk,) + lower]
+        for d in far_first(nx):
+            p = (me.x + d) % nx
+            remote(hx.at[p, y], bx1.at[me.x, y], xs1.at[p], xr1.at[me.x], me.on_x(p)).start()
+
+        @pl.when((c == 0) & (y != me.y))
+        def _():
+            remote(ha.at[y], ba1.at[me.a], as1.at[y], ar1.at[me.a], me.on_a(y)).start()
+
+        @pl.when(c == 1)
+        def _():
+            for d in far_first(n):
+                p = (me.a + d) % n
+                remote(ha.at[p, y], ba1.at[me.a, y], as1.at[p], ar1.at[me.a], me.on_a(p)).start()
+
+    def both(i, carry):
+        multiply(i, carry)
+        pass_on(i - n // 2)
+        return carry
+
+    def rest(i, carry):
+        pass_on(i)
         return carry
 
     lax.fori_loop(0, n // 2, multiply, 0)
@@ -178,23 +244,72 @@
         p = (me.a + d) % n
         send(hg.at[p], g1.at[me.a], gs1.at[d], gr1.at[me.a], me.on_a(p))
     g1[me.a] = hg[me.a]
-    lax.fori_loop(n // 2, n, multiply, 0)
-
-    def fill(y, carry):
-        arrived(rc.at[pl.ds(y * nx, nx)], cpair_r.at[y])
-        for x in range(nx):
-            blk = y * nx + x
-            for q in range(8):
-                rt, lh = q // 2, q % 2
-                z, t = q // tz, q % tz
-                at = (pl.ds(8 * rt, 8), pl.ds(LANES * lh, LANES))
-                h[y + c * (z - y), x, z + c * (y - z), t] = cross[(blk, c) + at] + rc[(blk,) + at]
-        return carry
-
-    lax.fori_loop(0, n, fill, 0)
-    for d in far_first(n):
-        p = (me.a + d) % n
-        send(h.at[p], b1.at[me.a], cs1.at[d], cr1.at[me.a], me.on_a(p))
+    lax.fori_loop(n // 2, n, both, 0)
+    lax.fori_loop(n // 2, n, rest, 0)
+
+    def sum_first():
+        for d in near_first(nx):
+            p = (me.x + d) % nx
+            arrived(bx1.at[p], xr1.at[p])
+
+        def add_x(p, carry):
+            for r in range(n):
+                y, z = p + c * (r - p), r + c * (p - r)
+                total = hx[me.x, y, z]
+                for d in range(1, nx):
+                    total = total + bx1[(me.x + d) % nx, y, z]
+                sx[p, r] = total
+            return carry
+
+        lax.fori_loop(0, n, add_x, 0)
+        for d in far_first(n):
+            p = (me.a + d) % n
+            send(sx.at[p], bx2.at[me.a], xs2.at[d], xr2.at[me.a], me.on_a(p))
+        for d in near_first(n):
+            p = (me.a + d) % n
+            arrived(ba1.at[p], ar1.at[p])
+
+        def add_a(r, carry):
+            for x in range(nx):
+                total = ha[me.a, r, x]
+                for d in range(1, n):
+                    total = total + ba1[(me.a + d) % n, r, x]
+                sa[x, r] = total
+            return carry
+
+        lax.fori_loop(0, n, add_a, 0)
+        for d in far_first(nx):
+            p = (me.x + d) % nx
+            send(sa.at[p], ba2.at[me.x], as2.at[d], ar2.at[me.x], me.on_x(p))
+
+    def sum_second():
+        total = sa[me.x]
+        for d in near_first(nx):
+            p = (me.x + d) % nx
+            arrived(ba2.at[p], ar2.at[p])
+            total = total + ba2[p]
+        s2[:, :, 4:8, :] = total
+        total = sx[me.a]
+        for d in near_first(n):
+            p = (me.a + d) % n
+            arrived(bx2.at[p], xr2.at[p])
+            total = total + bx2[p]
+        s2[:, :, 0:4, :] = total
+        for d in far_first(n):
+            p = (me.b + d) % n
+            send(s2.at[p], b3.at[me.b], cs3.at[d], cr3.at[me.b], me.on_b(p))
+
+    mine = pl.ds(me.z * tz, tz)
+
+    def sum_third():
+        total = s2[me.b]
+        for d in near_first(n):
+            p = (me.b + d) % n
+            arrived(b3.at[p], cr3.at[p])
+            total = total + b3[p]
+        csum[mine] = total
+        for d in far_first(n):
+            send(csum.at[mine], csum.at[mine], cs4.at[d], cr4.at[me.z], me.on_z((me.z + d) % n))
 
     for d in near_first(n):
         p = (me.a + d) % n
@@ -208,6 +323,7 @@
     g3[me.b] = sum_slots(g2, nx)
     for d in far_first(n):
         send(g3.at[me.b], g3.at[me.b], gs3.at[d], gr3.at[me.b], me.on_b((me.b + d) % n))
+    sum_first()
     for d in near_first(n):
         p = (me.b + d) % n
         arrived(g3.at[p], gr3.at[p])
@@ -219,6 +335,7 @@
     for d in far_first(n):
         send(gsum.at[owned(me.a)], gsum.at[owned(me.a)], gs4.at[d], gr4.at[me.a], me.on_a((me.a + d) % n))
     send(gsum.at[owned(me.a)], gsum.at[owned(me.a)], gs5.at[me.a], gr5.at[me.a], me.partner())
+    sum_second()
     for d in near_first(n):
         p = (me.a + d) % n
         arrived(gsum.at[owned(p)], gr4.at[p])
@@ -226,46 +343,6 @@
     for p in range(n):
         arrived(gsum.at[pl.ds((1 - c) * half + p * gt, gt)], gr5.at[p])
 
-    def sum_a():
-        for d in near_first(n):
-            p = (me.a + d) % n
-            arrived(b1.at[p], cr1.at[p])
-
-        def add(x, carry):
-            total = h[me.a, x]
-            for d in range(1, n):
-                total = total + b1[(me.a + d) % n, x]
-            s1[x] = total
-            return carry
-
-        lax.fori_loop(0, nx, add, 0)
-        for d in far_first(nx):
-            p = (me.x + d) % nx
-            send(s1.at[p], b2.at[me.x], cs2.at[d], cr2.at[me.x], me.on_x(p))
-
-    def sum_x():
-        total = s1[me.x]
-        for d in near_first(nx):
-            p = (me.x + d) % nx
-            arrived(b2.at[p], cr2.at[p])
-            total = total + b2[p]
-        s2[...] = total
-        for d in far_first(n):
-            p = (me.b + d) % n
-            send(s2.at[p], b3.at[me.b], cs3.at[d], cr3.at[me.b], me.on_b(p))
-
-    mine = pl.ds(me.z * tz, tz)
-
-    def sum_b():
-        total = s2[me.b]
-        for d in near_first(n):
-            p = (me.b + d) % n
-            arrived(b3.at[p], cr3.at[p])
-            total = total + b3[p]
-        csum[mine] = total
-        for d in far_first(n):
-            send(csum.at[mine], csum.at[mine], cs4.at[d], cr4.at[me.z], me.on_z((me.z + d) % n))
-
     lanes = lax.broadcasted_iota(jnp.int32, (8, 128), 1)
     subs = lax.broadcasted_iota(jnp.int32, (8, 128), 0)
 
@@ -273,7 +350,7 @@
         values = jnp.broadcast_to(ridge_ref[0:1, start:start + 128], (8, 128))
         return tile + jnp.where(lanes == subs + 8 * g, values, 0.0)
 
-    chol_block([ridged(gsum[g], g, 0) for g in range(16)], fac_ref, v_ref, 0, first_hooks(sum_a, sum_x, sum_b))
+    chol_block([ridged(gsum[g], g, 0) for g in range(16)], fac_ref, v_ref, 0, {4: sum_third})
     v11 = v_ref[0:128, 0:128]
     u12 = mm(v11, gsum[16:32].reshape(128, 128))
     fac_ref[0:128, 128:256] = u12
@@ -282,7 +359,7 @@
     q_ref[0] = mm(u12, u12, 0, 0)
     q_ref[1] = mm(u12, v11, 0, 0)
     trailing = [ridged(gsum[32 + g], g, 128) - q_ref[0, pl.ds(8 * g, 8), :] for g in range(16)]
-    chol_block(trailing, fac_ref, v_ref, 128, second_hooks(sum_a, sum_x, sum_b))
+    chol_block(trailing, fac_ref, v_ref, 128, {})
     v_ref[128:256, 0:128] = -mm(v_ref[128:256, 128:256], q_ref[1])
 
     for d in near_first(n):
@@ -298,16 +375,14 @@
         return carry
 
     lax.fori_loop(0, n, sent, 0)
+    for d in range(1, nx):
+        p = (me.x + d) % nx
+        remote(hx.at[p], bx1.at[me.x], xs1.at[p], xr1.at[me.x], me.on_x(p)).wait_send()
+    for d in range(1, n):
+        p = (me.a + d) % n
+        remote(ha.at[p], ba1.at[me.a], as1.at[p], ar1.at[me.a], me.on_a(p)).wait_send()
     for copy in sends:
         copy.wait_send()
-
-
-def first_hooks(sum_a, sum_x, sum_b):
-    return {2: sum_a, 13: sum_x}
-
-
-def second_hooks(sum_a, sum_x, sum_b):
-    return {6: sum_b}
 
 
 def ridge_call(n, nx, features, targets, ridge):
@@ -315,6 +390,7 @@
     rows = features.shape[0]
     f32 = lambda *shape: pltpu.VMEM(shape, jnp.float32)
     tiles = lambda *lead: f32(*lead, 8, LANES)
+    halves = lambda *lead: f32(*lead, 4, LANES)
     dma = lambda k: pltpu.SemaphoreType.DMA((k,))
     one = pltpu.SemaphoreType.DMA
     vmem, hbm = pl.BlockSpec(memory_space=pltpu.VMEM), pl.BlockSpec(memory_space=pltpu.HBM)
@@ -330,10 +406,11 @@
             pltpu.VMEM((rows, 256), jnp.bfloat16), pltpu.VMEM((n, rows, nx * 64), jnp.bfloat16),
             f32(n * nx, 2, 32, 256), tiles(48), tiles(48), tiles(8), f32(256, 256), f32(2, 128, 128),
             f32(n * nx, 32, 256), tiles(24), tiles(n, gt), tiles(n, gt), tiles(nx, gt), tiles(n, gt),
-            tiles(n, nx, n, tz), tiles(n, nx, n, tz), tiles(nx, n, tz), tiles(nx, n, tz), tiles(n, tz), tiles(n, tz),
+            halves(nx, n, n, tz), halves(nx, n, n, tz), halves(n, n, tz), halves(n, n, tz),
+            halves(n, n, nx, tz), halves(n, n, nx, tz), halves(nx, n, tz), halves(nx, n, tz), tiles(n, tz), tiles(n, tz),
             dma(n + 1), one, one, dma(n), dma(n),
             dma(n), dma(n), dma(nx), dma(nx), dma(n), dma(n), dma(n), dma(n), dma(n), dma(n),
-            dma(n), dma(n), dma(nx), dma(nx), dma(n), dma(n), dma(n), dma(n),
+            dma(nx), dma(nx), dma(n), dma(n), dma(n), dma(n), dma(nx), dma(nx), dma(n), dma(n), dma(n), dma(n),
         ],
         compiler_params=pltpu.CompilerParams(collective_id=0, has_side_effects=True),
     )(features, targets, ridge)

time: 57.6 us -> 51.4 us (0.89)
  Pallas kernels: 53.7 us -> 47.5 us
    pallas_call x1, Pallas kernels: 53.7 us -> 47.5 us  [ridge_call(): pl.pallas_call(functools.partial(ridge_kernel, n, nx), out_shape=(jax.Sha...]
where the time goes in v3:
time: 51.4 us; the launch traced here: 51.2 us
  Pallas kernels  47.5 us (92%)
  local copies, waits for them, and re-layouts  3.04 us (6%)
  between operations  0.64 us (1%)
    pallas_call x1, Pallas kernels, ridge_call(): pl.pallas_call(functools.partial(ridge_kernel, n, nx), out_shape=(jax.Sha...  47.5 us
    unnamed x2, local copies, waits for them, and re-layouts  3.04 us

profile of v3, /device:TPU:1, one launch (start us, length us, event | category | flops | bytes accessed | tf_op | source)
XLA Modules:
  0.0 51.2 jit_solution(12833989779106659792)
XLA Ops:
  0.6 47.5 %shard_map.50 = (f32[32,256]{1,0:T(8,128)}, f32[256,256]{1,0:T(8,128)}) custom-call(bf16[1024,256]{1,0:T(8,128)(2,1)} %f_hbm.1, bf16[1024,2048]{1,0:T(8,128)(2,1)} %t_hbm.1, f32[1,256]{1,0:T(1,128)} %bitcast.1), custom_call_target="tpu_custom_call" | custom-call | tf_op jit(solution)/shard_map/pallas_call | solution.py:397
  48.1 1.4 %copy.7 = f32[32,256]{1,0:T(8,128)} copy(f32[32,256]{1,0:T(8,128)} %get-tuple-element.4) | data formatting | bytes 65536
  49.5 1.7 %copy.8 = f32[256,256]{1,0:T(8,128)} copy(f32[256,256]{1,0:T(8,128)} %get-tuple-element.5) | data formatting | bytes 524288

commit v4 on v3

--- a/solution.py
+++ b/solution.py
@@ -124,10 +124,10 @@
     return sorted(range(1, n), key=lambda d: min(d, n - d))
 
 
-def sum_slots(ref, count):
-    total = ref[0]
+def sum_slots(ref, count, part):
+    total = ref[0, part]
     for p in range(1, count):
-        total = total + ref[p]
+        total = total + ref[p, part]
     return total
 
 
@@ -141,7 +141,8 @@
 ):
     me = Place(n, nx)
     c = me.c
-    gt, tz, half = 24 // n, 8 // n, 24
+    gk, tz = 8 // n, 8 // n
+    parts = (pl.ds(0, 1), pl.ds(1, 2))
     width = nx * 64
     sends = []
 
@@ -180,11 +181,12 @@
     over_rows = (((0,), (0,)), ((), ()))
     load_features.wait()
     whole = lax.dot_general(feat[...], feat[...], over_rows, preferred_element_type=jnp.float32)
-    gram[0:16] = whole[0:128, 0:128].reshape(16, 8, LANES)
-    gram[16:32] = whole[0:128, 128:256].reshape(16, 8, LANES)
-    gram[32:48] = whole[128:256, 128:256].reshape(16, 8, LANES)
+    gram[0] = whole[0:128, 0:128].reshape(16, 8, LANES)
+    gram[1] = whole[0:128, 128:256].reshape(16, 8, LANES)
+    gram[2] = whole[128:256, 128:256].reshape(16, 8, LANES)
     pl.semaphore_wait(barrier, len(greet))
-    send(gram.at[pl.ds((1 - c) * half, half)], rg, gpair_s, gpair_r, me.partner())
+    for k, part in enumerate(parts):
+        send(gram.at[part, pl.ds((1 - c) * 8, 8)], rg.at[part], gpair_s.at[k], gpair_r.at[k], me.partner())
 
     def pair(y):
         at = pl.ds(y * nx, nx)
@@ -237,13 +239,14 @@
         return carry
 
     lax.fori_loop(0, n // 2, multiply, 0)
-    arrived(rg, gpair_r)
-    for p in range(n):
-        hg[p] = gram[pl.ds(c * half + p * gt, gt)] + rg[pl.ds(p * gt, gt)]
-    for d in far_first(n):
-        p = (me.a + d) % n
-        send(hg.at[p], g1.at[me.a], gs1.at[d], gr1.at[me.a], me.on_a(p))
-    g1[me.a] = hg[me.a]
+    for k, part in enumerate(parts):
+        arrived(rg.at[part], gpair_r.at[k])
+        for p in range(n):
+            hg[p, part] = gram[part, pl.ds(c * 8 + p * gk, gk)] + rg[part, pl.ds(p * gk, gk)]
+        for d in far_first(n):
+            p = (me.a + d) % n
+            send(hg.at[p, part], g1.at[me.a, part], gs1.at[k * n + d], gr1.at[k * n + me.a], me.on_a(p))
+        g1[me.a, part] = hg[me.a, part]
     lax.fori_loop(n // 2, n, both, 0)
     lax.fori_loop(n // 2, n, rest, 0)
 
@@ -311,38 +314,61 @@
         for d in far_first(n):
             send(csum.at[mine], csum.at[mine], cs4.at[d], cr4.at[me.z], me.on_z((me.z + d) % n))
 
-    for d in near_first(n):
-        p = (me.a + d) % n
-        arrived(g1.at[p], gr1.at[p])
-    g2[me.x] = sum_slots(g1, n)
-    for d in far_first(nx):
-        send(g2.at[me.x], g2.at[me.x], gs2.at[d], gr2.at[me.x], me.on_x((me.x + d) % nx))
-    for d in near_first(nx):
-        p = (me.x + d) % nx
-        arrived(g2.at[p], gr2.at[p])
-    g3[me.b] = sum_slots(g2, nx)
-    for d in far_first(n):
-        send(g3.at[me.b], g3.at[me.b], gs3.at[d], gr3.at[me.b], me.on_b((me.b + d) % n))
+    def over_x(k):
+        part = parts[k]
+        for d in near_first(n):
+            p = (me.a + d) % n
+            arrived(g1.at[p, part], gr1.at[k * n + p])
+        g2[me.x, part] = sum_slots(g1, n, part)
+        mine = g2.at[me.x, part]
+        for d in far_first(nx):
+            send(mine, mine, gs2.at[k * nx + d], gr2.at[k * nx + me.x], me.on_x((me.x + d) % nx))
+
+    def over_b(k):
+        part = parts[k]
+        for d in near_first(nx):
+            p = (me.x + d) % nx
+            arrived(g2.at[p, part], gr2.at[k * nx + p])
+        g3[me.b, part] = sum_slots(g2, nx, part)
+        mine = g3.at[me.b, part]
+        for d in far_first(n):
+            send(mine, mine, gs3.at[k * n + d], gr3.at[k * n + me.b], me.on_b((me.b + d) % n))
+
+    def owned(k, core, p):
+        return gsum.at[parts[k], pl.ds(core * 8 + p * gk, gk)]
+
+    def gather(k):
+        part = parts[k]
+        for d in near_first(n):
+            p = (me.b + d) % n
+            arrived(g3.at[p, part], gr3.at[k * n + p])
+        mine = owned(k, c, me.a)
+        mine[...] = sum_slots(g3, n, part)
+        for d in far_first(n):
+            send(mine, mine, gs4.at[k * n + d], gr4.at[k * n + me.a], me.on_a((me.a + d) % n))
+        send(mine, mine, gs5.at[k * n + me.a], gr5.at[k * n + me.a], me.partner())
+
+    def forward(k):
+        for d in near_first(n):
+            p = (me.a + d) % n
+            block = owned(k, c, p)
+            arrived(block, gr4.at[k * n + p])
+            send(block, block, gs5.at[k * n + p], gr5.at[k * n + p], me.partner())
+
+    def complete(k):
+        for p in range(n):
+            arrived(owned(k, 1 - c, p), gr5.at[k * n + p])
+
+    over_x(0)
+    over_x(1)
+    over_b(0)
+    over_b(1)
     sum_first()
-    for d in near_first(n):
-        p = (me.b + d) % n
-        arrived(g3.at[p], gr3.at[p])
-
-    def owned(p):
-        return pl.ds(c * half + p * gt, gt)
-
-    gsum[owned(me.a)] = sum_slots(g3, n)
-    for d in far_first(n):
-        send(gsum.at[owned(me.a)], gsum.at[owned(me.a)], gs4.at[d], gr4.at[me.a], me.on_a((me.a + d) % n))
-    send(gsum.at[owned(me.a)], gsum.at[owned(me.a)], gs5.at[me.a], gr5.at[me.a], me.partner())
+    gather(0)
+    gather(1)
     sum_second()
-    for d in near_first(n):
-        p = (me.a + d) % n
-        arrived(gsum.at[owned(p)], gr4.at[p])
-        send(gsum.at[owned(p)], gsum.at[owned(p)], gs5.at[p], gr5.at[p], me.partner())
-    for p in range(n):
-        arrived(gsum.at[pl.ds((1 - c) * half + p * gt, gt)], gr5.at[p])
-
+    forward(0)
+    complete(0)
     lanes = lax.broadcasted_iota(jnp.int32, (8, 128), 1)
     subs = lax.broadcasted_iota(jnp.int32, (8, 128), 0)
 
@@ -350,15 +376,16 @@
         values = jnp.broadcast_to(ridge_ref[0:1, start:start + 128], (8, 128))
         return tile + jnp.where(lanes == subs + 8 * g, values, 0.0)
 
-    chol_block([ridged(gsum[g], g, 0) for g in range(16)], fac_ref, v_ref, 0, {4: sum_third})
+    chol_block([ridged(gsum[0, g], g, 0) for g in range(16)], fac_ref, v_ref, 0, {1: lambda: forward(1), 2: sum_third})
+    complete(1)
     v11 = v_ref[0:128, 0:128]
-    u12 = mm(v11, gsum[16:32].reshape(128, 128))
+    u12 = mm(v11, gsum[1].reshape(128, 128))
     fac_ref[0:128, 128:256] = u12
     fac_ref[128:256, 0:128] = jnp.zeros((128, 128), jnp.float32)
     v_ref[0:128, 128:256] = jnp.zeros((128, 128), jnp.float32)
     q_ref[0] = mm(u12, u12, 0, 0)
     q_ref[1] = mm(u12, v11, 0, 0)
-    trailing = [ridged(gsum[32 + g], g, 128) - q_ref[0, pl.ds(8 * g, 8), :] for g in range(16)]
+    trailing = [ridged(gsum[2, g], g, 128) - q_ref[0, pl.ds(8 * g, 8), :] for g in range(16)]
     chol_block(trailing, fac_ref, v_ref, 128, {})
     v_ref[128:256, 0:128] = -mm(v_ref[128:256, 128:256], q_ref[1])
 
@@ -386,13 +413,12 @@
 
 
 def ridge_call(n, nx, features, targets, ridge):
-    gt, tz = 24 // n, 8 // n
+    gk, tz = 8 // n, 8 // n
     rows = features.shape[0]
     f32 = lambda *shape: pltpu.VMEM(shape, jnp.float32)
     tiles = lambda *lead: f32(*lead, 8, LANES)
     halves = lambda *lead: f32(*lead, 4, LANES)
     dma = lambda k: pltpu.SemaphoreType.DMA((k,))
-    one = pltpu.SemaphoreType.DMA
     vmem, hbm = pl.BlockSpec(memory_space=pltpu.VMEM), pl.BlockSpec(memory_space=pltpu.HBM)
     return pl.pallas_call(
         functools.partial(ridge_kernel, n, nx),
@@ -404,20 +430,51 @@
         out_specs=(vmem, vmem),
         scratch_shapes=[
             pltpu.VMEM((rows, 256), jnp.bfloat16), pltpu.VMEM((n, rows, nx * 64), jnp.bfloat16),
-            f32(n * nx, 2, 32, 256), tiles(48), tiles(48), tiles(8), f32(256, 256), f32(2, 128, 128),
-            f32(n * nx, 32, 256), tiles(24), tiles(n, gt), tiles(n, gt), tiles(nx, gt), tiles(n, gt),
+            f32(n * nx, 2, 32, 256), tiles(3, 16), tiles(3, 16), tiles(8), f32(256, 256), f32(2, 128, 128),
+            f32(n * nx, 32, 256), tiles(3, 8), tiles(n, 3, gk), tiles(n, 3, gk), tiles(nx, 3, gk), tiles(n, 3, gk),
             halves(nx, n, n, tz), halves(nx, n, n, tz), halves(n, n, tz), halves(n, n, tz),
             halves(n, n, nx, tz), halves(n, n, nx, tz), halves(nx, n, tz), halves(nx, n, tz), tiles(n, tz), tiles(n, tz),
-            dma(n + 1), one, one, dma(n), dma(n),
-            dma(n), dma(n), dma(nx), dma(nx), dma(n), dma(n), dma(n), dma(n), dma(n), dma(n),
+            dma(n + 1), dma(2), dma(2), dma(n), dma(n),
+            dma(2 * n), dma(2 * n), dma(2 * nx), dma(2 * nx), dma(2 * n), dma(2 * n), dma(2 * n), dma(2 * n), dma(2 * n), dma(2 * n),
             dma(nx), dma(nx), dma(n), dma(n), dma(n), dma(n), dma(nx), dma(nx), dma(n), dma(n), dma(n), dma(n),
         ],
         compiler_params=pltpu.CompilerParams(collective_id=0, has_side_effects=True),
     )(features, targets, ridge)
 
 
+def hand_kernel(read_in, fac_in, read_out, fac_out, read_v, fac_v, came, went):
+    chunk = 64
+    takes = [pltpu.make_async_copy(read_in, read_v, came.at[4])]
+    gives = [pltpu.make_async_copy(read_v, read_out, went.at[4])]
+    for k in range(4):
+        rows = pl.ds(chunk * k, chunk)
+        takes.append(pltpu.make_async_copy(fac_in.at[rows], fac_v.at[rows], came.at[k]))
+        gives.append(pltpu.make_async_copy(fac_v.at[rows], fac_out.at[rows], went.at[k]))
+    for take in takes:
+        take.start()
+    for take, give in zip(takes, gives):
+        take.wait()
+        give.start()
+    for give in gives:
+        give.wait()
+
+
+def hand_call(readout, factor):
+    hbm = pl.BlockSpec(memory_space=pltpu.HBM)
+    return pl.pallas_call(
+        hand_kernel,
+        out_shape=(jax.ShapeDtypeStruct((32, 256), jnp.float32), jax.ShapeDtypeStruct((256, 256), jnp.float32)),
+        in_specs=[hbm, hbm],
+        out_specs=(hbm, hbm),
+        scratch_shapes=[
+            pltpu.VMEM((32, 256), jnp.float32), pltpu.VMEM((256, 256), jnp.float32),
+            pltpu.SemaphoreType.DMA((5,)), pltpu.SemaphoreType.DMA((5,)),
+        ],
+    )(readout, factor)
+
+
 def shards(n, nx, features, targets, ridge):
-    return ridge_call(n, nx, features, targets, ridge.reshape(1, 256))
+    return hand_call(*ridge_call(n, nx, features, targets, ridge.reshape(1, 256)))
 
 
 def solution(mesh):

time: 51.4 us -> 49.7 us (0.967)
  local copies, waits for them, and re-layouts: 3.04 us -> 0 us
  Pallas kernels: 47.5 us -> 48.9 us
    unnamed x2 -> x0, local copies, waits for them, and re-layouts: 3.04 us -> none
    pallas_call x0 -> x1, Pallas kernels: none -> 1.67 us  [hand_call(): pl.pallas_call(hand_kernel, out_shape=(jax.ShapeDtypeStruct((32, 256), jn...]
where the time goes in v4:
time: 49.7 us; the launch traced here: 49.5 us
  Pallas kernels  48.9 us (98%)
  between operations  0.64 us (1%)
    pallas_call x1, Pallas kernels, ridge_call(): pl.pallas_call(functools.partial(ridge_kernel, n, nx), out_shape=(jax.Sha...  47.2 us
    pallas_call x1, Pallas kernels, hand_call(): pl.pallas_call(hand_kernel, out_shape=(jax.ShapeDtypeStruct((32, 256), jn...  1.67 us

profile of v4, /device:TPU:1, one launch (start us, length us, event | category | flops | bytes accessed | tf_op | source)
XLA Modules:
  0.0 49.5 jit_solution(1402476303299509529)
XLA Ops:
  0.6 47.2 %shard_map.50 = (f32[32,256]{1,0:T(8,128)}, f32[256,256]{1,0:T(8,128)}) custom-call(bf16[1024,256]{1,0:T(8,128)(2,1)} %f_hbm.1, bf16[1024,2048]{1,0:T(8,128)(2,1)} %t_hbm.1, f32[1,256]{1,0:T(1,128)} %bitcast.1), custom_call_target="tpu_custom_call" | custom-call | tf_op jit(solution)/shard_map/pallas_call | solution.py:423
  47.9 1.7 %shard_map.51 = (f32[32,256]{1,0:T(8,128)}, f32[256,256]{1,0:T(8,128)}) custom-call(f32[32,256]{1,0:T(8,128)} %get-tuple-element.4.read_in, f32[256,256]{1,0:T(8,128)} %get-tuple-element.5.fac_in), custom_call_target="tpu_custom_call" | custom-call | tf_op jit(solution)/shard_map/pallas_call | solution.py:464

commit v5 on v4

--- a/solution.py
+++ b/solution.py
@@ -383,11 +383,14 @@
     fac_ref[0:128, 128:256] = u12
     fac_ref[128:256, 0:128] = jnp.zeros((128, 128), jnp.float32)
     v_ref[0:128, 128:256] = jnp.zeros((128, 128), jnp.float32)
-    q_ref[0] = mm(u12, u12, 0, 0)
-    q_ref[1] = mm(u12, v11, 0, 0)
-    trailing = [ridged(gsum[2, g], g, 128) - q_ref[0, pl.ds(8 * g, 8), :] for g in range(16)]
-    chol_block(trailing, fac_ref, v_ref, 128, {})
-    v_ref[128:256, 0:128] = -mm(v_ref[128:256, 128:256], q_ref[1])
+    square = mm(u12, u12, 0, 0)
+
+    def corner():
+        q_ref[...] = mm(u12, v11, 0, 0)
+
+    trailing = [ridged(gsum[2, g], g, 128) - square[8 * g:8 * g + 8, :] for g in range(16)]
+    chol_block(trailing, fac_ref, v_ref, 128, {4: corner})
+    v_ref[128:256, 0:128] = -mm(v_ref[128:256, 128:256], q_ref[...])
 
     for d in near_first(n):
         p = (me.z + d) % n
@@ -430,7 +433,7 @@
         out_specs=(vmem, vmem),
         scratch_shapes=[
             pltpu.VMEM((rows, 256), jnp.bfloat16), pltpu.VMEM((n, rows, nx * 64), jnp.bfloat16),
-            f32(n * nx, 2, 32, 256), tiles(3, 16), tiles(3, 16), tiles(8), f32(256, 256), f32(2, 128, 128),
+            f32(n * nx, 2, 32, 256), tiles(3, 16), tiles(3, 16), tiles(8), f32(256, 256), f32(128, 128),
             f32(n * nx, 32, 256), tiles(3, 8), tiles(n, 3, gk), tiles(n, 3, gk), tiles(nx, 3, gk), tiles(n, 3, gk),
             halves(nx, n, n, tz), halves(nx, n, n, tz), halves(n, n, tz), halves(n, n, tz),
             halves(n, n, nx, tz), halves(n, n, nx, tz), halves(nx, n, tz), halves(nx, n, tz), tiles(n, tz), tiles(n, tz),

time: 49.7 us -> 49.7 us (level)
  no operation moved by 1% of the time
where the time goes in v5:
time: 49.7 us; the launch traced here: 49.5 us
  Pallas kernels  48.9 us (98%)
  between operations  0.64 us (1%)
    pallas_call x1, Pallas kernels, ridge_call(): pl.pallas_call(functools.partial(ridge_kernel, n, nx), out_shape=(jax.Sha...  47.2 us
    pallas_call x1, Pallas kernels, hand_call(): pl.pallas_call(hand_kernel, out_shape=(jax.ShapeDtypeStruct((32, 256), jn...  1.67 us

profile of v5, /device:TPU:1, one launch (start us, length us, event | category | flops | bytes accessed | tf_op | source)
XLA Modules:
  0.0 49.5 jit_solution(1402476303299509529)
XLA Ops:
  0.6 47.2 %shard_map.50 = (f32[32,256]{1,0:T(8,128)}, f32[256,256]{1,0:T(8,128)}) custom-call(bf16[1024,256]{1,0:T(8,128)(2,1)} %f_hbm.1, bf16[1024,2048]{1,0:T(8,128)(2,1)} %t_hbm.1, f32[1,256]{1,0:T(1,128)} %bitcast.1), custom_call_target="tpu_custom_call" | custom-call | tf_op jit(solution)/shard_map/pallas_call | solution.py:426
  47.9 1.7 %shard_map.51 = (f32[32,256]{1,0:T(8,128)}, f32[256,256]{1,0:T(8,128)}) custom-call(f32[32,256]{1,0:T(8,128)} %get-tuple-element.4.read_in, f32[256,256]{1,0:T(8,128)} %get-tuple-element.5.fac_in), custom_call_target="tpu_custom_call" | custom-call | tf_op jit(solution)/shard_map/pallas_call | solution.py:467
